TPU v7x, 256 devices: a whole 4x4x8 slice. The times are simulated.
256 devices in a mesh: leaf: 64 (over z, x, core), sub: 4 (over y).
Axes of the slice: x: 4, y: 4, z: 8, core: 2. Of those that a mesh axis runs over, the one named last changes fastest.
Arguments:
- coords: bfloat16 [32768, 3, 128], P('leaf'), may hold values from 0 to 4
- charges: bfloat16 [32768, 8, 128], P(('leaf', 'sub')), may hold values from -6 to 6
- counts: int32 [32768], P('leaf'), may hold values from 32 to 128, as said below
- morton: int32 [32768], P('leaf'), may hold values from 0 to 511, as said below
- near_list: int32 [32768, 27], P(('leaf', 'sub')), may hold values from -1 to 32767, as said below
- basis: bfloat16 [32768, 64, 128], P(('leaf', 'sub')), may hold values from -0.5 to 0.5
- transfer1: bfloat16 [32768, 64, 64], P(('leaf', 'sub')), may hold values from -0.75 to 0.75
- far2_list: int32 [4096, 16], P(('leaf', 'sub')), may hold values from -1 to 4095, as said below
- coupling2: bfloat16 [4096, 16, 64, 64], P(('leaf', 'sub')), may hold values from -0.0625 to 0.0625
- transfer2: bfloat16 [4096, 64, 64], P('leaf'), may hold values from -0.75 to 0.75
- far3_list: int32 [64, 8], P('leaf'), may hold values from -1 to 63, as said below
- coupling3: bfloat16 [64, 8, 64, 64], P('leaf'), may hold values from -0.01171875 to 0.01171875
Outputs:
- potential: float32 [32768, 8, 128], P(('leaf', 'sub'))
Inputs may be any that keep to these rules, and one draw needn't show every extreme that they name: `counts`: each leaf's number of live points; leaves do not all have the same number. `morton`: within every block of 512 consecutive entries, a permutation of 0 to 511. `near_list`: row t starts with t itself; its other live entries are leaves other than t in the leaf group of t or in the group just before or after it; live entries come first and -1 fills the rest, with at least 13 live entries a row; entries may repeat. `far2_list`: row b names boxes other than b in the leaf group of b or in the group just before or after it; live entries come first and -1 fills the rest, with at least 8 live entries a row; entries may repeat. `far3_list`: row q names group boxes other than q; live entries come first and -1 fills the rest, with at least 4 live entries a row; entries may repeat.
All inputs are finite; a program needn't handle non-finite values.
Results may differ from a plain program's by a relative error of at most 0.011.
Values may be sent and summed in bfloat16 or wider, within the bound.
No kernel may reach another device: no remote copies, remote signals or barrier semaphores. Data moves between devices by JAX's collectives and lax.ppermute only.
A program may use at most 64 MiB of HBM per device.

v0:
```python
import jax
import jax.numpy as jnp
from jax import lax
from jax.sharding import PartitionSpec as P

kernel_scale = 0.07957747154594767
delta_squared = 0.0025


def with_halo(cells, sides, width):
    for axis, dim in sides:
        count = lax.axis_size(axis)
        ends = count - 1
        head = lax.slice_in_dim(cells, 0, width, axis=dim)
        tail = lax.slice_in_dim(cells, cells.shape[dim] - width, cells.shape[dim], axis=dim)
        cells = jnp.concatenate(
            [
                lax.ppermute(tail, axis, [(i, (i + 1) % count) for i in range(ends)]),
                cells,
                lax.ppermute(head, axis, [((i + 1) % count, i) for i in range(ends)]),
            ],
            axis=dim,
        )
    return cells


def kernel_tile(targets, sources):
    squared = jnp.zeros((targets.shape[0], targets.shape[2], sources.shape[2]), jnp.float32)
    for component in range(3):
        offset = targets[:, component, :, None] - sources[:, component, None, :]
        squared = squared + offset * offset
    return (kernel_scale / jnp.sqrt(squared + delta_squared)).astype(jnp.bfloat16)


def far_field(moments, lists, couplings, offset):
    valid = lists >= 0
    local = jnp.clip(lists - offset, 0, moments.shape[0] - 1)
    source = jnp.where(valid[..., None, None], moments[local], jnp.zeros((), moments.dtype))
    return jnp.einsum("bkrc,bkcp->brp", source, couplings, preferred_element_type=jnp.float32)


def on_device(
    coords,
    charges,
    counts,
    morton,
    near_list,
    basis,
    transfer1,
    far2_list,
    coupling2,
    transfer2,
    far3_list,
    coupling3,
):
    lane = lax.axis_index("sub")
    group = lax.axis_index("leaf")
    leaf_dev = charges.shape[0]
    rhs_count = charges.shape[1]
    points = charges.shape[2]
    rank_size = basis.shape[1]
    group_size = coords.shape[0]
    clusters = far2_list.shape[0]
    group_boxes = transfer2.shape[0]
    start = lane * leaf_dev
    arrived = lax.all_gather(charges, "sub", axis=0, tiled=True)
    inverse = (
        jnp.zeros((group_size,), jnp.int32).at[morton].set(jnp.arange(group_size, dtype=jnp.int32))
    )
    ordered = arrived[inverse]
    live = jnp.arange(points, dtype=jnp.int32)[None, :] < counts[:, None]
    masked = jnp.where(live[:, None, :], ordered, jnp.zeros((), ordered.dtype))
    packed = jnp.concatenate([coords, masked], axis=1)
    nearby = with_halo(packed, (("leaf", 0),), group_size)
    own_charges = lax.dynamic_slice_in_dim(masked, start, leaf_dev, 0)
    own_live = lax.dynamic_slice_in_dim(live, start, leaf_dev, 0)
    targets = lax.dynamic_slice_in_dim(coords, start, leaf_dev, 0).astype(jnp.float32)
    transfer_boxed = transfer1.reshape(clusters, 8, rank_size, rank_size)
    leaf_moments = jnp.einsum(
        "trp,tkp->trk", own_charges, basis, preferred_element_type=jnp.float32
    ).astype(jnp.bfloat16)
    box_moments = jnp.einsum(
        "bnrc,bncp->brp",
        leaf_moments.reshape(clusters, 8, rhs_count, rank_size),
        transfer_boxed,
        preferred_element_type=jnp.float32,
    ).astype(jnp.bfloat16)
    group_moments = lax.all_gather(box_moments, "sub", axis=0, tiled=True)
    top_moment = jnp.einsum(
        "brc,bcp->rp", group_moments, transfer2, preferred_element_type=jnp.float32
    ).astype(jnp.bfloat16)
    all_top = lax.all_gather(top_moment[None], "leaf", axis=0, tiled=True)
    near_boxes = with_halo(group_moments, (("leaf", 0),), group_boxes)
    top_field = far_field(all_top, far3_list, coupling3, 0).astype(jnp.bfloat16)
    box_far = far_field(near_boxes, far2_list, coupling2, (group - 1) * group_boxes)
    own_transfer = lax.dynamic_slice_in_dim(transfer2, lane * clusters, clusters, 0)
    box_local = (
        box_far
        + jnp.einsum("rp,bcp->brc", top_field[0], own_transfer, preferred_element_type=jnp.float32)
    ).astype(jnp.bfloat16)
    leaf_local = jnp.einsum(
        "brp,bncp->bnrc", box_local, transfer_boxed, preferred_element_type=jnp.float32
    ).astype(jnp.bfloat16)
    leaf_local = leaf_local.reshape(leaf_dev, rhs_count, rank_size)
    far_part = jnp.einsum("trk,tkp->trp", leaf_local, basis, preferred_element_type=jnp.float32)
    base = (group - 1) * group_size

    def slot_step(total, column):
        valid = column >= 0
        index = jnp.clip(column - base, 0, 3 * group_size - 1)
        rows = nearby[index]
        tile = kernel_tile(targets, rows[:, :3].astype(jnp.float32))
        source = jnp.where(valid[:, None, None], rows[:, 3:], jnp.zeros((), rows.dtype))
        return (
            total + jnp.einsum("tij,trj->tri", tile, source, preferred_element_type=jnp.float32),
            None,
        )

    near_part, unused = lax.scan(
        slot_step, jnp.zeros((leaf_dev, rhs_count, points), jnp.float32), near_list.T
    )
    return jnp.where(own_live[:, None, :], near_part + far_part, jnp.zeros((), jnp.float32))


def solution(mesh):
    return jax.shard_map(
        on_device,
        mesh=mesh,
        in_specs=(
            P("leaf", None, None),
            P(("leaf", "sub"), None, None),
            P("leaf"),
            P("leaf"),
            P(("leaf", "sub"), None),
            P(("leaf", "sub"), None, None),
            P(("leaf", "sub"), None, None),
            P(("leaf", "sub"), None),
            P(("leaf", "sub"), None, None, None),
            P("leaf", None, None),
            P("leaf", None),
            P("leaf", None, None, None),
        ),
        out_specs=P(("leaf", "sub"), None, None),
        check_vma=False,
    )
```

profile of v0, /device:TPU:1, one launch (start us, length us, event | category | flops | bytes accessed | tf_op | source)
XLA Modules:
  0.0 683.8 jit_solution(16244068060757462938)
XLA Ops:
  11.1 4.8 copy.23
  19.3 19.4 %all-gather.3.cloned.1.call-done = bf16[512,8,128]{2,1,0:T(8,128)(2,1)} async-done(((bf16[128,8,128]{2,1,0:T(8,128)(2,1)}), bf16[512,8,128]{2,1,0:T(8,128)(2,1)}) %all-gather.3.cloned.1.call-update) | async-done | bytes 1048592 | tf_op jit(solution)/shard_map/all_gather | solution.py:66
  45.3 9.5 %all_gather.10 = bf16[64,8,64]{2,1,0:T(8,128)(2,1)S(1)} all-gather(bf16[16,8,64]{2,1,0:T(8,128)(2,1)S(1)} %fusion.10), channel_id=1, replica_groups=mesh['leaf'=64,'sub'=4] {'sub'}, dimensions={0}, use_global_device_ids=true | all-gather | bytes 81920 | tf_op jit(solution)/shard_map/all_gather | solution.py:88
  54.8 7.1 %collective-permute-start.2 = (bf16[64,8,64]{2,1,0:T(8,128)(2,1)S(1)}, bf16[64,8,64]{2,1,0:T(8,128)(2,1)}, u32[]{:S(2)}, u32[]{:S(2)}) collective-permute-start(bf16[64,8,64]{2,1,0:T(8,128)(2,1)S(1)} %all_gather.10), channel_id=1, source_target_pairs={{0,4},{4,8},{8,12},{12,16},{16,20},{20,24},{24,28},{28,32},{32,36}... | collective-permute-start | bytes 196616 | tf_op jit(solution)/shard_map/ppermute | solution.py:18
  66.2 3.6 collective-permute-start
  72.1 72.7 %all-gather = bf16[512,64]{1,0:T(8,128)(2,1)} all-gather(bf16[8,64]{1,0:T(8,128)(2,1)S(1)} %fusion.12), channel_id=2, replica_groups=mesh['leaf'=64,'sub'=4] {'leaf'}, dimensions={0}, use_global_device_ids=true | all-gather | bytes 66560 | tf_op jit(solution)/shard_map/all_gather | solution.py:92
  151.8 3.5 convolution_bitcast_fusion.1
  155.4 4.3 convolution_convert_fusion
  167.0 25.8 %pad_maximum_fusion = bf16[1536,11,128]{2,1,0:T(8,128)(2,1)} fusion(bf16[512,11,128]{2,1,0:T(8,128)(2,1)S(1)} %copy.22, bf16[512,8,128]{2,1,0:T(8,128)(2,1)S(1)} %broadcast_select_fusion, bf16[512,3,128]{2,1,0:T(4,128)(2,1)S(1)} %copy-done.3, bf16[512,11,128]{2,1,0:T(8,128)(2,1)S(1)} %copy.21), kind=kLoop, calls=%fused_computation.23 | loop fusion | flops 17301504 | bytes 8650752 | tf_op jit(solution)/shard_map/concatenate | solution.py:16
  192.7 482.2 %while.11 = (s32[]{:T(128)}, f32[128,8,128]{2,1,0:T(8,128)}, s32[27,128]{1,0:T(8,128)}, s32[]{:T(128)}, bf16[1536,11,128]{2,1,0:T(8,128)(2,1)}, /*index=5*/f32[128,3,128]{2,0,1:T(8,128)S(1)}, s32[]{:T(128)}, s32[]{:T(128)}) while((s32[]{:T(128)}, f32[128,8,128]{2,1,0:T(8,128)}, s32[27,128]{1,0:T(8,128)}, s32[]{:T(128)}, ...), condition=%wide.region_2.3_spmd.clone, body=%wide.region_1.2_spmd.clone.sunk | while | flops 57067264 | bytes 3513195 | solution.py:119
  193.5 3.5 gather_fusion
  199.1 11.5 %fusion.50 = f32[128,8,128]{2,1,0:T(8,128)} fusion(f32[128,128]{1,0:T(8,128)S(1)} %bitcast.93, f32[128,128]{1,0:T(8,128)} %get-tuple-element.121, f32[128,128]{1,0:T(8,128)S(1)} %bitcast.94, f32[128,128]{1,0:T(8,128)} %get-tuple-element.123, f32[128,128]{1,0:T(8,128)S(1)} %bitcast.92, f32[128,128]{1,0:T(8,128)} %get-tuple-element.125, ...), kind=kOutput, calls=%fused_computation.7.clone.1 | convolution fusion | flops 57016320 | bytes 1704065 | tf_op jit(solution)/shard_map/while/body/eval_jaxpr/tij,trj->tri/dot_general | solution.py:115
  211.3 3.5 gather_fusion
  216.9 11.6 %fusion.50 = f32[128,8,128]{2,1,0:T(8,128)} fusion(f32[128,128]{1,0:T(8,128)S(1)} %bitcast.93, f32[128,128]{1,0:T(8,128)} %get-tuple-element.121, f32[128,128]{1,0:T(8,128)S(1)} %bitcast.94, f32[128,128]{1,0:T(8,128)} %get-tuple-element.123, f32[128,128]{1,0:T(8,128)S(1)} %bitcast.92, f32[128,128]{1,0:T(8,128)} %get-tuple-element.125, ...), kind=kOutput, calls=%fused_computation.7.clone.1 | convolution fusion | flops 57016320 | bytes 1704065 | tf_op jit(solution)/shard_map/while/body/eval_jaxpr/tij,trj->tri/dot_general | solution.py:115
  229.2 3.5 gather_fusion
  234.7 11.6 %fusion.50 = f32[128,8,128]{2,1,0:T(8,128)} fusion(f32[128,128]{1,0:T(8,128)S(1)} %bitcast.93, f32[128,128]{1,0:T(8,128)} %get-tuple-element.121, f32[128,128]{1,0:T(8,128)S(1)} %bitcast.94, f32[128,128]{1,0:T(8,128)} %get-tuple-element.123, f32[128,128]{1,0:T(8,128)S(1)} %bitcast.92, f32[128,128]{1,0:T(8,128)} %get-tuple-element.125, ...), kind=kOutput, calls=%fused_computation.7.clone.1 | convolution fusion | flops 57016320 | bytes 1704065 | tf_op jit(solution)/shard_map/while/body/eval_jaxpr/tij,trj->tri/dot_general | solution.py:115
  252.6 11.6 %fusion.50 = f32[128,8,128]{2,1,0:T(8,128)} fusion(f32[128,128]{1,0:T(8,128)S(1)} %bitcast.93, f32[128,128]{1,0:T(8,128)} %get-tuple-element.121, f32[128,128]{1,0:T(8,128)S(1)} %bitcast.94, f32[128,128]{1,0:T(8,128)} %get-tuple-element.123, f32[128,128]{1,0:T(8,128)S(1)} %bitcast.92, f32[128,128]{1,0:T(8,128)} %get-tuple-element.125, ...), kind=kOutput, calls=%fused_computation.7.clone.1 | convolution fusion | flops 57016320 | bytes 1704065 | tf_op jit(solution)/shard_map/while/body/eval_jaxpr/tij,trj->tri/dot_general | solution.py:115
  270.5 11.6 %fusion.50 = f32[128,8,128]{2,1,0:T(8,128)} fusion(f32[128,128]{1,0:T(8,128)S(1)} %bitcast.93, f32[128,128]{1,0:T(8,128)} %get-tuple-element.121, f32[128,128]{1,0:T(8,128)S(1)} %bitcast.94, f32[128,128]{1,0:T(8,128)} %get-tuple-element.123, f32[128,128]{1,0:T(8,128)S(1)} %bitcast.92, f32[128,128]{1,0:T(8,128)} %get-tuple-element.125, ...), kind=kOutput, calls=%fused_computation.7.clone.1 | convolution fusion | flops 57016320 | bytes 1704065 | tf_op jit(solution)/shard_map/while/body/eval_jaxpr/tij,trj->tri/dot_general | solution.py:115
  282.7 3.5 gather_fusion
  288.3 11.6 %fusion.50 = f32[128,8,128]{2,1,0:T(8,128)} fusion(f32[128,128]{1,0:T(8,128)S(1)} %bitcast.93, f32[128,128]{1,0:T(8,128)} %get-tuple-element.121, f32[128,128]{1,0:T(8,128)S(1)} %bitcast.94, f32[128,128]{1,0:T(8,128)} %get-tuple-element.123, f32[128,128]{1,0:T(8,128)S(1)} %bitcast.92, f32[128,128]{1,0:T(8,128)} %get-tuple-element.125, ...), kind=kOutput, calls=%fused_computation.7.clone.1 | convolution fusion | flops 57016320 | bytes 1704065 | tf_op jit(solution)/shard_map/while/body/eval_jaxpr/tij,trj->tri/dot_general | solution.py:115
  300.6 3.5 gather_fusion
  306.2 11.6 %fusion.50 = f32[128,8,128]{2,1,0:T(8,128)} fusion(f32[128,128]{1,0:T(8,128)S(1)} %bitcast.93, f32[128,128]{1,0:T(8,128)} %get-tuple-element.121, f32[128,128]{1,0:T(8,128)S(1)} %bitcast.94, f32[128,128]{1,0:T(8,128)} %get-tuple-element.123, f32[128,128]{1,0:T(8,128)S(1)} %bitcast.92, f32[128,128]{1,0:T(8,128)} %get-tuple-element.125, ...), kind=kOutput, calls=%fused_computation.7.clone.1 | convolution fusion | flops 57016320 | bytes 1704065 | tf_op jit(solution)/shard_map/while/body/eval_jaxpr/tij,trj->tri/dot_general | solution.py:115
  318.5 3.5 gather_fusion
  324.1 11.6 %fusion.50 = f32[128,8,128]{2,1,0:T(8,128)} fusion(f32[128,128]{1,0:T(8,128)S(1)} %bitcast.93, f32[128,128]{1,0:T(8,128)} %get-tuple-element.121, f32[128,128]{1,0:T(8,128)S(1)} %bitcast.94, f32[128,128]{1,0:T(8,128)} %get-tuple-element.123, f32[128,128]{1,0:T(8,128)S(1)} %bitcast.92, f32[128,128]{1,0:T(8,128)} %get-tuple-element.125, ...), kind=kOutput, calls=%fused_computation.7.clone.1 | convolution fusion | flops 57016320 | bytes 1704065 | tf_op jit(solution)/shard_map/while/body/eval_jaxpr/tij,trj->tri/dot_general | solution.py:115
  341.9 11.6 %fusion.50 = f32[128,8,128]{2,1,0:T(8,128)} fusion(f32[128,128]{1,0:T(8,128)S(1)} %bitcast.93, f32[128,128]{1,0:T(8,128)} %get-tuple-element.121, f32[128,128]{1,0:T(8,128)S(1)} %bitcast.94, f32[128,128]{1,0:T(8,128)} %get-tuple-element.123, f32[128,128]{1,0:T(8,128)S(1)} %bitcast.92, f32[128,128]{1,0:T(8,128)} %get-tuple-element.125, ...), kind=kOutput, calls=%fused_computation.7.clone.1 | convolution fusion | flops 57016320 | bytes 1704065 | tf_op jit(solution)/shard_map/while/body/eval_jaxpr/tij,trj->tri/dot_general | solution.py:115
  359.8 11.6 %fusion.50 = f32[128,8,128]{2,1,0:T(8,128)} fusion(f32[128,128]{1,0:T(8,128)S(1)} %bitcast.93, f32[128,128]{1,0:T(8,128)} %get-tuple-element.121, f32[128,128]{1,0:T(8,128)S(1)} %bitcast.94, f32[128,128]{1,0:T(8,128)} %get-tuple-element.123, f32[128,128]{1,0:T(8,128)S(1)} %bitcast.92, f32[128,128]{1,0:T(8,128)} %get-tuple-element.125, ...), kind=kOutput, calls=%fused_computation.7.clone.1 | convolution fusion | flops 57016320 | bytes 1704065 | tf_op jit(solution)/shard_map/while/body/eval_jaxpr/tij,trj->tri/dot_general | solution.py:115
  372.1 3.5 gather_fusion
  377.6 11.6 %fusion.50 = f32[128,8,128]{2,1,0:T(8,128)} fusion(f32[128,128]{1,0:T(8,128)S(1)} %bitcast.93, f32[128,128]{1,0:T(8,128)} %get-tuple-element.121, f32[128,128]{1,0:T(8,128)S(1)} %bitcast.94, f32[128,128]{1,0:T(8,128)} %get-tuple-element.123, f32[128,128]{1,0:T(8,128)S(1)} %bitcast.92, f32[128,128]{1,0:T(8,128)} %get-tuple-element.125, ...), kind=kOutput, calls=%fused_computation.7.clone.1 | convolution fusion | flops 57016320 | bytes 1704065 | tf_op jit(solution)/shard_map/while/body/eval_jaxpr/tij,trj->tri/dot_general | solution.py:115
  389.9 3.5 gather_fusion
  395.5 11.6 %fusion.50 = f32[128,8,128]{2,1,0:T(8,128)} fusion(f32[128,128]{1,0:T(8,128)S(1)} %bitcast.93, f32[128,128]{1,0:T(8,128)} %get-tuple-element.121, f32[128,128]{1,0:T(8,128)S(1)} %bitcast.94, f32[128,128]{1,0:T(8,128)} %get-tuple-element.123, f32[128,128]{1,0:T(8,128)S(1)} %bitcast.92, f32[128,128]{1,0:T(8,128)} %get-tuple-element.125, ...), kind=kOutput, calls=%fused_computation.7.clone.1 | convolution fusion | flops 57016320 | bytes 1704065 | tf_op jit(solution)/shard_map/while/body/eval_jaxpr/tij,trj->tri/dot_general | solution.py:115
  407.8 3.5 gather_fusion
  413.4 11.6 %fusion.50 = f32[128,8,128]{2,1,0:T(8,128)} fusion(f32[128,128]{1,0:T(8,128)S(1)} %bitcast.93, f32[128,128]{1,0:T(8,128)} %get-tuple-element.121, f32[128,128]{1,0:T(8,128)S(1)} %bitcast.94, f32[128,128]{1,0:T(8,128)} %get-tuple-element.123, f32[128,128]{1,0:T(8,128)S(1)} %bitcast.92, f32[128,128]{1,0:T(8,128)} %get-tuple-element.125, ...), kind=kOutput, calls=%fused_computation.7.clone.1 | convolution fusion | flops 57016320 | bytes 1704065 | tf_op jit(solution)/shard_map/while/body/eval_jaxpr/tij,trj->tri/dot_general | solution.py:115
  425.7 3.5 gather_fusion
  431.2 11.6 %fusion.50 = f32[128,8,128]{2,1,0:T(8,128)} fusion(f32[128,128]{1,0:T(8,128)S(1)} %bitcast.93, f32[128,128]{1,0:T(8,128)} %get-tuple-element.121, f32[128,128]{1,0:T(8,128)S(1)} %bitcast.94, f32[128,128]{1,0:T(8,128)} %get-tuple-element.123, f32[128,128]{1,0:T(8,128)S(1)} %bitcast.92, f32[128,128]{1,0:T(8,128)} %get-tuple-element.125, ...), kind=kOutput, calls=%fused_computation.7.clone.1 | convolution fusion | flops 57016320 | bytes 1704065 | tf_op jit(solution)/shard_map/while/body/eval_jaxpr/tij,trj->tri/dot_general | solution.py:115
  449.1 11.6 %fusion.50 = f32[128,8,128]{2,1,0:T(8,128)} fusion(f32[128,128]{1,0:T(8,128)S(1)} %bitcast.93, f32[128,128]{1,0:T(8,128)} %get-tuple-element.121, f32[128,128]{1,0:T(8,128)S(1)} %bitcast.94, f32[128,128]{1,0:T(8,128)} %get-tuple-element.123, f32[128,128]{1,0:T(8,128)S(1)} %bitcast.92, f32[128,128]{1,0:T(8,128)} %get-tuple-element.125, ...), kind=kOutput, calls=%fused_computation.7.clone.1 | convolution fusion | flops 57016320 | bytes 1704065 | tf_op jit(solution)/shard_map/while/body/eval_jaxpr/tij,trj->tri/dot_general | solution.py:115
  467.0 11.6 %fusion.50 = f32[128,8,128]{2,1,0:T(8,128)} fusion(f32[128,128]{1,0:T(8,128)S(1)} %bitcast.93, f32[128,128]{1,0:T(8,128)} %get-tuple-element.121, f32[128,128]{1,0:T(8,128)S(1)} %bitcast.94, f32[128,128]{1,0:T(8,128)} %get-tuple-element.123, f32[128,128]{1,0:T(8,128)S(1)} %bitcast.92, f32[128,128]{1,0:T(8,128)} %get-tuple-element.125, ...), kind=kOutput, calls=%fused_computation.7.clone.1 | convolution fusion | flops 57016320 | bytes 1704065 | tf_op jit(solution)/shard_map/while/body/eval_jaxpr/tij,trj->tri/dot_general | solution.py:115
  484.8 11.6 %fusion.50 = f32[128,8,128]{2,1,0:T(8,128)} fusion(f32[128,128]{1,0:T(8,128)S(1)} %bitcast.93, f32[128,128]{1,0:T(8,128)} %get-tuple-element.121, f32[128,128]{1,0:T(8,128)S(1)} %bitcast.94, f32[128,128]{1,0:T(8,128)} %get-tuple-element.123, f32[128,128]{1,0:T(8,128)S(1)} %bitcast.92, f32[128,128]{1,0:T(8,128)} %get-tuple-element.125, ...), kind=kOutput, calls=%fused_computation.7.clone.1 | convolution fusion | flops 57016320 | bytes 1704065 | tf_op jit(solution)/shard_map/while/body/eval_jaxpr/tij,trj->tri/dot_general | solution.py:115
  502.7 11.6 %fusion.50 = f32[128,8,128]{2,1,0:T(8,128)} fusion(f32[128,128]{1,0:T(8,128)S(1)} %bitcast.93, f32[128,128]{1,0:T(8,128)} %get-tuple-element.121, f32[128,128]{1,0:T(8,128)S(1)} %bitcast.94, f32[128,128]{1,0:T(8,128)} %get-tuple-element.123, f32[128,128]{1,0:T(8,128)S(1)} %bitcast.92, f32[128,128]{1,0:T(8,128)} %get-tuple-element.125, ...), kind=kOutput, calls=%fused_computation.7.clone.1 | convolution fusion | flops 57016320 | bytes 1704065 | tf_op jit(solution)/shard_map/while/body/eval_jaxpr/tij,trj->tri/dot_general | solution.py:115
  515.0 3.5 gather_fusion
  520.5 11.6 %fusion.50 = f32[128,8,128]{2,1,0:T(8,128)} fusion(f32[128,128]{1,0:T(8,128)S(1)} %bitcast.93, f32[128,128]{1,0:T(8,128)} %get-tuple-element.121, f32[128,128]{1,0:T(8,128)S(1)} %bitcast.94, f32[128,128]{1,0:T(8,128)} %get-tuple-element.123, f32[128,128]{1,0:T(8,128)S(1)} %bitcast.92, f32[128,128]{1,0:T(8,128)} %get-tuple-element.125, ...), kind=kOutput, calls=%fused_computation.7.clone.1 | convolution fusion | flops 57016320 | bytes 1704065 | tf_op jit(solution)/shard_map/while/body/eval_jaxpr/tij,trj->tri/dot_general | solution.py:115
  538.4 11.6 %fusion.50 = f32[128,8,128]{2,1,0:T(8,128)} fusion(f32[128,128]{1,0:T(8,128)S(1)} %bitcast.93, f32[128,128]{1,0:T(8,128)} %get-tuple-element.121, f32[128,128]{1,0:T(8,128)S(1)} %bitcast.94, f32[128,128]{1,0:T(8,128)} %get-tuple-element.123, f32[128,128]{1,0:T(8,128)S(1)} %bitcast.92, f32[128,128]{1,0:T(8,128)} %get-tuple-element.125, ...), kind=kOutput, calls=%fused_computation.7.clone.1 | convolution fusion | flops 57016320 | bytes 1704065 | tf_op jit(solution)/shard_map/while/body/eval_jaxpr/tij,trj->tri/dot_general | solution.py:115
  556.3 11.6 %fusion.50 = f32[128,8,128]{2,1,0:T(8,128)} fusion(f32[128,128]{1,0:T(8,128)S(1)} %bitcast.93, f32[128,128]{1,0:T(8,128)} %get-tuple-element.121, f32[128,128]{1,0:T(8,128)S(1)} %bitcast.94, f32[128,128]{1,0:T(8,128)} %get-tuple-element.123, f32[128,128]{1,0:T(8,128)S(1)} %bitcast.92, f32[128,128]{1,0:T(8,128)} %get-tuple-element.125, ...), kind=kOutput, calls=%fused_computation.7.clone.1 | convolution fusion | flops 57016320 | bytes 1704065 | tf_op jit(solution)/shard_map/while/body/eval_jaxpr/tij,trj->tri/dot_general | solution.py:115
  574.1 11.6 %fusion.50 = f32[128,8,128]{2,1,0:T(8,128)} fusion(f32[128,128]{1,0:T(8,128)S(1)} %bitcast.93, f32[128,128]{1,0:T(8,128)} %get-tuple-element.121, f32[128,128]{1,0:T(8,128)S(1)} %bitcast.94, f32[128,128]{1,0:T(8,128)} %get-tuple-element.123, f32[128,128]{1,0:T(8,128)S(1)} %bitcast.92, f32[128,128]{1,0:T(8,128)} %get-tuple-element.125, ...), kind=kOutput, calls=%fused_computation.7.clone.1 | convolution fusion | flops 57016320 | bytes 1704065 | tf_op jit(solution)/shard_map/while/body/eval_jaxpr/tij,trj->tri/dot_general | solution.py:115
  592.0 11.6 %fusion.50 = f32[128,8,128]{2,1,0:T(8,128)} fusion(f32[128,128]{1,0:T(8,128)S(1)} %bitcast.93, f32[128,128]{1,0:T(8,128)} %get-tuple-element.121, f32[128,128]{1,0:T(8,128)S(1)} %bitcast.94, f32[128,128]{1,0:T(8,128)} %get-tuple-element.123, f32[128,128]{1,0:T(8,128)S(1)} %bitcast.92, f32[128,128]{1,0:T(8,128)} %get-tuple-element.125, ...), kind=kOutput, calls=%fused_computation.7.clone.1 | convolution fusion | flops 57016320 | bytes 1704065 | tf_op jit(solution)/shard_map/while/body/eval_jaxpr/tij,trj->tri/dot_general | solution.py:115
  609.8 11.6 %fusion.50 = f32[128,8,128]{2,1,0:T(8,128)} fusion(f32[128,128]{1,0:T(8,128)S(1)} %bitcast.93, f32[128,128]{1,0:T(8,128)} %get-tuple-element.121, f32[128,128]{1,0:T(8,128)S(1)} %bitcast.94, f32[128,128]{1,0:T(8,128)} %get-tuple-element.123, f32[128,128]{1,0:T(8,128)S(1)} %bitcast.92, f32[128,128]{1,0:T(8,128)} %get-tuple-element.125, ...), kind=kOutput, calls=%fused_computation.7.clone.1 | convolution fusion | flops 57016320 | bytes 1704065 | tf_op jit(solution)/shard_map/while/body/eval_jaxpr/tij,trj->tri/dot_general | solution.py:115
  627.7 11.6 %fusion.50 = f32[128,8,128]{2,1,0:T(8,128)} fusion(f32[128,128]{1,0:T(8,128)S(1)} %bitcast.93, f32[128,128]{1,0:T(8,128)} %get-tuple-element.121, f32[128,128]{1,0:T(8,128)S(1)} %bitcast.94, f32[128,128]{1,0:T(8,128)} %get-tuple-element.123, f32[128,128]{1,0:T(8,128)S(1)} %bitcast.92, f32[128,128]{1,0:T(8,128)} %get-tuple-element.125, ...), kind=kOutput, calls=%fused_computation.7.clone.1 | convolution fusion | flops 57016320 | bytes 1704065 | tf_op jit(solution)/shard_map/while/body/eval_jaxpr/tij,trj->tri/dot_general | solution.py:115
  645.6 11.6 %fusion.50 = f32[128,8,128]{2,1,0:T(8,128)} fusion(f32[128,128]{1,0:T(8,128)S(1)} %bitcast.93, f32[128,128]{1,0:T(8,128)} %get-tuple-element.121, f32[128,128]{1,0:T(8,128)S(1)} %bitcast.94, f32[128,128]{1,0:T(8,128)} %get-tuple-element.123, f32[128,128]{1,0:T(8,128)S(1)} %bitcast.92, f32[128,128]{1,0:T(8,128)} %get-tuple-element.125, ...), kind=kOutput, calls=%fused_computation.7.clone.1 | convolution fusion | flops 57016320 | bytes 1704065 | tf_op jit(solution)/shard_map/while/body/eval_jaxpr/tij,trj->tri/dot_general | solution.py:115
  663.4 11.6 %fusion.50 = f32[128,8,128]{2,1,0:T(8,128)} fusion(f32[128,128]{1,0:T(8,128)S(1)} %bitcast.93, f32[128,128]{1,0:T(8,128)} %get-tuple-element.121, f32[128,128]{1,0:T(8,128)S(1)} %bitcast.94, f32[128,128]{1,0:T(8,128)} %get-tuple-element.123, f32[128,128]{1,0:T(8,128)S(1)} %bitcast.92, f32[128,128]{1,0:T(8,128)} %get-tuple-element.125, ...), kind=kOutput, calls=%fused_computation.7.clone.1 | convolution fusion | flops 57016320 | bytes 1704065 | tf_op jit(solution)/shard_map/while/body/eval_jaxpr/tij,trj->tri/dot_general | solution.py:115
  (236 shorter events, 168.1 us)
Async XLA Ops:
  6.5 37.1 %copy-start = (bf16[128,64,128]{2,1,0:T(8,128)(2,1)S(1)}, bf16[128,64,128]{2,1,0:T(8,128)(2,1)}, u32[]{:S(2)}) copy-start(bf16[128,64,128]{2,1,0:T(8,128)(2,1)} %param.19) | copy-start | bytes 6291460
  6.5 12.7 %copy-start.6 = (s32[16,16]{1,0:T(8,128)S(1)}, s32[16,16]{1,0:T(8,128)}, u32[]{:S(2)}) copy-start(s32[16,16]{1,0:T(8,128)} %param.21) | copy-start | bytes 3076
  6.5 11.6 %copy-start.8 = (s32[1,8]{1,0:T(1,128)S(1)}, s32[1,8]{1,0:T(1,128)}, u32[]{:S(2)}) copy-start(s32[1,8]{1,0:T(1,128)} %param.24) | copy-start | bytes 100
  6.5 11.6 %copy-start.7 = (s32[512]{0:T(512)S(1)}, s32[512]{0:T(512)}, u32[]{:S(2)}) copy-start(s32[512]{0:T(512)} %param.16) | copy-start | bytes 6148
  6.5 32.1 %all-gather.3.cloned.1.call-start = ((), (), s32[]{:S(2)}) async-start(), calls=%async_computation | async-start | bytes 1310720 | tf_op jit(solution)/shard_map/all_gather | solution.py:66
  42.0 2.9 copy-start.1
  42.0 21.9 %copy-start.2 = (bf16[512,3,128]{2,1,0:T(4,128)(2,1)S(1)}, bf16[512,3,128]{2,1,0:T(4,128)(2,1)}, u32[]{:S(2)}) copy-start(bf16[512,3,128]{2,1,0:T(4,128)(2,1)} %copy.18) | copy-start | bytes 1179652
  45.3 26.5 %copy-start.5 = (bf16[64,64,64]{2,1,0:T(8,128)(2,1)S(1)}, bf16[64,64,64]{2,1,0:T(8,128)(2,1)}, u32[]{:S(2)}) copy-start(bf16[64,64,64]{2,1,0:T(8,128)(2,1)} %param.23) | copy-start | bytes 1572868
  54.8 92.6 %collective-permute-start.2 = (bf16[64,8,64]{2,1,0:T(8,128)(2,1)S(1)}, bf16[64,8,64]{2,1,0:T(8,128)(2,1)}, u32[]{:S(2)}, u32[]{:S(2)}) collective-permute-start(bf16[64,8,64]{2,1,0:T(8,128)(2,1)S(1)} %all_gather.10), channel_id=1, source_target_pairs={{0,4},{4,8},{8,12},{12,16},{16,20},{20,24},{24,28},{28,32},{32,36}... | collective-permute-start | bytes 196616 | tf_op jit(solution)/shard_map/ppermute | solution.py:18
  62.0 85.5 %collective-permute-start.3 = (bf16[64,8,64]{2,1,0:T(8,128)(2,1)S(1)}, bf16[64,8,64]{2,1,0:T(8,128)(2,1)}, u32[]{:S(2)}, u32[]{:S(2)}) collective-permute-start(bf16[64,8,64]{2,1,0:T(8,128)(2,1)S(1)} %all_gather.10), channel_id=1, source_target_pairs={{4,0},{8,4},{12,8},{16,12},{20,16},{24,20},{28,24},{32,28},{36,32}... | collective-permute-start | bytes 196616 | tf_op jit(solution)/shard_map/ppermute | solution.py:20
  66.2 95.9 %collective-permute-start = (bf16[512,11,128]{2,0,1:T(8,128)(2,1)}, bf16[512,11,128]{2,0,1:T(8,128)(2,1)}, u32[]{:S(2)}, u32[]{:S(2)}) collective-permute-start(bf16[512,11,128]{2,0,1:T(8,128)(2,1)} %copy.19), channel_id=1, source_target_pairs={{0,4},{4,8},{8,12},{12,16},{16,20},{20,24},{24,28},{28,32},{32,36}... | collective-permute-start | bytes 4325384 | tf_op jit(solution)/shard_map/ppermute | solution.py:18
  69.9 94.7 %collective-permute-start.1 = (bf16[512,11,128]{2,0,1:T(8,128)(2,1)}, bf16[512,11,128]{2,0,1:T(8,128)(2,1)}, u32[]{:S(2)}, u32[]{:S(2)}) collective-permute-start(bf16[512,11,128]{2,0,1:T(8,128)(2,1)} %copy.19), channel_id=1, source_target_pairs={{4,0},{8,4},{12,8},{16,12},{20,16},{24,20},{28,24},{32,28},{36,32}... | collective-permute-start | bytes 4325384 | tf_op jit(solution)/shard_map/ppermute | solution.py:20
  162.1 4.8 copy-start.3
  192.7 482.2 %copy-start.4 = (f32[128,8,128]{2,1,0:T(8,128)S(1)}, f32[128,8,128]{2,1,0:T(8,128)}, u32[]{:S(2)}) copy-start(f32[128,8,128]{2,1,0:T(8,128)} %fusion.34) | copy-start | bytes 1572868
Sparse Core Ops, SparseCore 0:
  9.2 29.4 all-gather.2
where the time goes:
time: 689 us; the launch traced here: 684 us
  matrix products  325 us (47%)
  local copies, waits for them, and re-layouts  140 us (20%)
  other arithmetic  87.3 us (13%)
  blocking collectives  82.3 us (12%)
  waiting for transfers between devices  20.1 us (3%)
  starting transfers between devices  14.7 us (2%)
  between operations  13.6 us (2%)
    dot_general x27, matrix products, slot_step(): jnp.einsum('tij,trj->tri', tile, source, preferred_element_type=jnp.float32)  312 us
    gather x27, local copies, waits for them, and re-layouts, slot_step(): rows = nearby[index]  94.2 us
    all_gather x1, blocking collectives, on_device(): all_top = lax.all_gather(top_moment[None], 'leaf', axis=0, tiled=True)  72.7 us
    ge x27, other arithmetic, slot_step(): valid = column >= 0  32.9 us
    concatenate x2, other arithmetic, with_halo(): jnp.concatenate([lax.ppermute(tail, axis, [(i, (i + 1) % count) for i in...  27.6 us
    all_gather x1, waiting for transfers between devices, on_device(): arrived = lax.all_gather(charges, 'sub', axis=0, tiled=True)  19.4 us
    select_n x27, other arithmetic, slot_step(): rows = nearby[index]  19 us
    sub x27, local copies, waits for them, and re-layouts, kernel_tile(): offset = targets[:, component, :, None] - sources[:, component, None, :]  18.6 us
  transfers between devices with their start and end apart: 5, of which 1 were waited for; matrix products, arithmetic and copies ran while one was open for 5% of the time, Pallas kernels for 0%

commit v1 on v0

--- a/solution.py
+++ b/solution.py
@@ -63,7 +63,31 @@
     clusters = far2_list.shape[0]
     group_boxes = transfer2.shape[0]
     start = lane * leaf_dev
-    arrived = lax.all_gather(charges, "sub", axis=0, tiled=True)
+    carry_out, m_next, w2 = (lax.axis_size("sub"), lax.axis_index("sub"), charges.shape[0])
+    arrived = lax.dynamic_update_slice_in_dim(
+        jnp.zeros(
+            tuple((w * carry_out if ix == 0 else w for ix, w in enumerate(charges.shape))),
+            charges.dtype,
+        ),
+        charges,
+        m_next * w2,
+        axis=0,
+    )
+    met_up = y1 = charges
+    for dev_i in [*range(1, carry_out // 2 + 1)]:
+        met_up = lax.ppermute(
+            met_up, "sub", tuple(((ix, (ix + 1) % carry_out) for ix in range(carry_out)))
+        )
+        arrived = lax.dynamic_update_slice_in_dim(
+            arrived, met_up, (m_next - dev_i) % carry_out * w2, axis=0
+        )
+        if 2 * dev_i < carry_out:
+            y1 = lax.ppermute(
+                y1, "sub", tuple(((ix, (ix - 1) % carry_out) for ix in range(carry_out)))
+            )
+            arrived = lax.dynamic_update_slice_in_dim(
+                arrived, y1, (m_next + dev_i) % carry_out * w2, axis=0
+            )
     inverse = (
         jnp.zeros((group_size,), jnp.int32).at[morton].set(jnp.arange(group_size, dtype=jnp.int32))
     )

time: 689 us -> 668 us (0.970)
  waiting for transfers between devices: 20.1 us -> 0.02 us
  between operations: 13.6 us -> 0.29 us
    all_gather x1 -> x0, waiting for transfers between devices: 19.4 us -> none  [on_device(): arrived = lax.all_gather(charges, 'sub', axis=0, tiled=True)]
  transfers between devices with their start and end apart: 5 -> 7, of which waited for: 1 -> 0; matrix products, arithmetic and copies ran while one was open for 5% -> 6% of each run, Pallas kernels for 0% -> 0%
where the time goes in v1:
time: 668 us; the launch traced here: 662 us
  matrix products  325 us (49%)
  local copies, waits for them, and re-layouts  143 us (21%)
  other arithmetic  91.3 us (14%)
  blocking collectives  83.3 us (12%)
  starting transfers between devices  18.6 us (3%)
    dot_general x27, matrix products, slot_step(): jnp.einsum('tij,trj->tri', tile, source, preferred_element_type=jnp.float32)  312 us
    gather x27, local copies, waits for them, and re-layouts, slot_step(): rows = nearby[index]  94.2 us
    all_gather x1, blocking collectives, on_device(): all_top = lax.all_gather(top_moment[None], 'leaf', axis=0, tiled=True)  74 us
    ge x27, other arithmetic, slot_step(): valid = column >= 0  34.5 us
    concatenate x2, other arithmetic, with_halo(): jnp.concatenate([lax.ppermute(tail, axis, [(i, (i + 1) % count) for i in...  27.3 us
    select_n x27, other arithmetic, slot_step(): rows = nearby[index]  19 us
    sub x27, local copies, waits for them, and re-layouts, kernel_tile(): offset = targets[:, component, :, None] - sources[:, component, None, :]  18.5 us
  transfers between devices with their start and end apart: 7, of which 0 were waited for; matrix products, arithmetic and copies ran while one was open for 6% of the time, Pallas kernels for 0%

profile of v1, /device:TPU:1, one launch (start us, length us, event | category | flops | bytes accessed | tf_op | source)
XLA Modules:
  0.0 662.4 jit_solution(1097964356635547423)
XLA Ops:
  14.8 4.7 copy.23
  28.2 9.3 %all_gather.6 = bf16[64,8,64]{2,1,0:T(8,128)(2,1)S(1)} all-gather(bf16[16,8,64]{2,1,0:T(8,128)(2,1)S(1)} %fusion.10), channel_id=1, replica_groups=mesh['leaf'=64,'sub'=4] {'sub'}, dimensions={0}, use_global_device_ids=true | all-gather | bytes 81920 | tf_op jit(solution)/shard_map/all_gather | solution.py:112
  37.6 7.4 %collective-permute-start.5 = (bf16[64,8,64]{2,1,0:T(8,128)(2,1)S(1)}, bf16[64,8,64]{2,1,0:T(8,128)(2,1)}, u32[]{:S(2)}, u32[]{:S(2)}) collective-permute-start(bf16[64,8,64]{2,1,0:T(8,128)(2,1)S(1)} %all_gather.6), channel_id=1, source_target_pairs={{0,4},{4,8},{8,12},{12,16},{16,20},{20,24},{24,28},{28,32},{32,36}... | collective-permute-start | bytes 196616 | tf_op jit(solution)/shard_map/ppermute | solution.py:18
  49.4 3.5 collective-permute-start.3
  55.1 74.0 %all-gather = bf16[512,64]{1,0:T(8,128)(2,1)} all-gather(bf16[8,64]{1,0:T(8,128)(2,1)S(1)} %fusion.12), channel_id=2, replica_groups=mesh['leaf'=64,'sub'=4] {'leaf'}, dimensions={0}, use_global_device_ids=true | all-gather | bytes 66560 | tf_op jit(solution)/shard_map/all_gather | solution.py:116
  136.1 3.5 convolution_bitcast_fusion.1
  139.7 4.3 convolution_convert_fusion
  151.2 25.5 %pad_maximum_fusion = bf16[1536,11,128]{2,1,0:T(8,128)(2,1)} fusion(bf16[512,11,128]{2,1,0:T(8,128)(2,1)S(1)} %copy.22, bf16[512,8,128]{2,1,0:T(8,128)(2,1)S(1)} %broadcast_select_fusion, bf16[512,3,128]{2,1,0:T(4,128)(2,1)S(1)} %copy-done.3, bf16[512,11,128]{2,1,0:T(8,128)(2,1)S(1)} %copy.21), kind=kLoop, calls=%fused_computation.23 | loop fusion | flops 17301504 | bytes 8650752 | tf_op jit(solution)/shard_map/concatenate | solution.py:16
  176.8 483.7 %while.11 = (s32[]{:T(128)}, f32[128,8,128]{2,1,0:T(8,128)}, s32[27,128]{1,0:T(8,128)}, s32[]{:T(128)}, bf16[1536,11,128]{2,1,0:T(8,128)(2,1)}, /*index=5*/f32[128,3,128]{2,0,1:T(8,128)S(1)}, s32[]{:T(128)}, s32[]{:T(128)}) while((s32[]{:T(128)}, f32[128,8,128]{2,1,0:T(8,128)}, s32[27,128]{1,0:T(8,128)}, s32[]{:T(128)}, ...), condition=%wide.region_2.3_spmd.clone, body=%wide.region_1.2_spmd.clone.sunk | while | flops 57067264 | bytes 3513195 | solution.py:143
  177.5 3.5 gather_fusion
  183.2 11.5 %fusion.50 = f32[128,8,128]{2,1,0:T(8,128)} fusion(f32[128,128]{1,0:T(8,128)S(1)} %bitcast.93, f32[128,128]{1,0:T(8,128)} %get-tuple-element.121, f32[128,128]{1,0:T(8,128)S(1)} %bitcast.94, f32[128,128]{1,0:T(8,128)} %get-tuple-element.123, f32[128,128]{1,0:T(8,128)S(1)} %bitcast.92, f32[128,128]{1,0:T(8,128)} %get-tuple-element.125, ...), kind=kOutput, calls=%fused_computation.7.clone.1 | convolution fusion | flops 57016320 | bytes 1704065 | tf_op jit(solution)/shard_map/while/body/eval_jaxpr/tij,trj->tri/dot_general | solution.py:139
  195.4 3.5 gather_fusion
  201.0 11.6 %fusion.50 = f32[128,8,128]{2,1,0:T(8,128)} fusion(f32[128,128]{1,0:T(8,128)S(1)} %bitcast.93, f32[128,128]{1,0:T(8,128)} %get-tuple-element.121, f32[128,128]{1,0:T(8,128)S(1)} %bitcast.94, f32[128,128]{1,0:T(8,128)} %get-tuple-element.123, f32[128,128]{1,0:T(8,128)S(1)} %bitcast.92, f32[128,128]{1,0:T(8,128)} %get-tuple-element.125, ...), kind=kOutput, calls=%fused_computation.7.clone.1 | convolution fusion | flops 57016320 | bytes 1704065 | tf_op jit(solution)/shard_map/while/body/eval_jaxpr/tij,trj->tri/dot_general | solution.py:139
  213.3 3.5 gather_fusion
  218.9 11.6 %fusion.50 = f32[128,8,128]{2,1,0:T(8,128)} fusion(f32[128,128]{1,0:T(8,128)S(1)} %bitcast.93, f32[128,128]{1,0:T(8,128)} %get-tuple-element.121, f32[128,128]{1,0:T(8,128)S(1)} %bitcast.94, f32[128,128]{1,0:T(8,128)} %get-tuple-element.123, f32[128,128]{1,0:T(8,128)S(1)} %bitcast.92, f32[128,128]{1,0:T(8,128)} %get-tuple-element.125, ...), kind=kOutput, calls=%fused_computation.7.clone.1 | convolution fusion | flops 57016320 | bytes 1704065 | tf_op jit(solution)/shard_map/while/body/eval_jaxpr/tij,trj->tri/dot_general | solution.py:139
  236.9 11.6 %fusion.50 = f32[128,8,128]{2,1,0:T(8,128)} fusion(f32[128,128]{1,0:T(8,128)S(1)} %bitcast.93, f32[128,128]{1,0:T(8,128)} %get-tuple-element.121, f32[128,128]{1,0:T(8,128)S(1)} %bitcast.94, f32[128,128]{1,0:T(8,128)} %get-tuple-element.123, f32[128,128]{1,0:T(8,128)S(1)} %bitcast.92, f32[128,128]{1,0:T(8,128)} %get-tuple-element.125, ...), kind=kOutput, calls=%fused_computation.7.clone.1 | convolution fusion | flops 57016320 | bytes 1704065 | tf_op jit(solution)/shard_map/while/body/eval_jaxpr/tij,trj->tri/dot_general | solution.py:139
  254.8 11.6 %fusion.50 = f32[128,8,128]{2,1,0:T(8,128)} fusion(f32[128,128]{1,0:T(8,128)S(1)} %bitcast.93, f32[128,128]{1,0:T(8,128)} %get-tuple-element.121, f32[128,128]{1,0:T(8,128)S(1)} %bitcast.94, f32[128,128]{1,0:T(8,128)} %get-tuple-element.123, f32[128,128]{1,0:T(8,128)S(1)} %bitcast.92, f32[128,128]{1,0:T(8,128)} %get-tuple-element.125, ...), kind=kOutput, calls=%fused_computation.7.clone.1 | convolution fusion | flops 57016320 | bytes 1704065 | tf_op jit(solution)/shard_map/while/body/eval_jaxpr/tij,trj->tri/dot_general | solution.py:139
  267.1 3.5 gather_fusion
  272.7 11.6 %fusion.50 = f32[128,8,128]{2,1,0:T(8,128)} fusion(f32[128,128]{1,0:T(8,128)S(1)} %bitcast.93, f32[128,128]{1,0:T(8,128)} %get-tuple-element.121, f32[128,128]{1,0:T(8,128)S(1)} %bitcast.94, f32[128,128]{1,0:T(8,128)} %get-tuple-element.123, f32[128,128]{1,0:T(8,128)S(1)} %bitcast.92, f32[128,128]{1,0:T(8,128)} %get-tuple-element.125, ...), kind=kOutput, calls=%fused_computation.7.clone.1 | convolution fusion | flops 57016320 | bytes 1704065 | tf_op jit(solution)/shard_map/while/body/eval_jaxpr/tij,trj->tri/dot_general | solution.py:139
  285.0 3.5 gather_fusion
  290.6 11.6 %fusion.50 = f32[128,8,128]{2,1,0:T(8,128)} fusion(f32[128,128]{1,0:T(8,128)S(1)} %bitcast.93, f32[128,128]{1,0:T(8,128)} %get-tuple-element.121, f32[128,128]{1,0:T(8,128)S(1)} %bitcast.94, f32[128,128]{1,0:T(8,128)} %get-tuple-element.123, f32[128,128]{1,0:T(8,128)S(1)} %bitcast.92, f32[128,128]{1,0:T(8,128)} %get-tuple-element.125, ...), kind=kOutput, calls=%fused_computation.7.clone.1 | convolution fusion | flops 57016320 | bytes 1704065 | tf_op jit(solution)/shard_map/while/body/eval_jaxpr/tij,trj->tri/dot_general | solution.py:139
  302.9 3.5 gather_fusion
  308.5 11.6 %fusion.50 = f32[128,8,128]{2,1,0:T(8,128)} fusion(f32[128,128]{1,0:T(8,128)S(1)} %bitcast.93, f32[128,128]{1,0:T(8,128)} %get-tuple-element.121, f32[128,128]{1,0:T(8,128)S(1)} %bitcast.94, f32[128,128]{1,0:T(8,128)} %get-tuple-element.123, f32[128,128]{1,0:T(8,128)S(1)} %bitcast.92, f32[128,128]{1,0:T(8,128)} %get-tuple-element.125, ...), kind=kOutput, calls=%fused_computation.7.clone.1 | convolution fusion | flops 57016320 | bytes 1704065 | tf_op jit(solution)/shard_map/while/body/eval_jaxpr/tij,trj->tri/dot_general | solution.py:139
  326.4 11.6 %fusion.50 = f32[128,8,128]{2,1,0:T(8,128)} fusion(f32[128,128]{1,0:T(8,128)S(1)} %bitcast.93, f32[128,128]{1,0:T(8,128)} %get-tuple-element.121, f32[128,128]{1,0:T(8,128)S(1)} %bitcast.94, f32[128,128]{1,0:T(8,128)} %get-tuple-element.123, f32[128,128]{1,0:T(8,128)S(1)} %bitcast.92, f32[128,128]{1,0:T(8,128)} %get-tuple-element.125, ...), kind=kOutput, calls=%fused_computation.7.clone.1 | convolution fusion | flops 57016320 | bytes 1704065 | tf_op jit(solution)/shard_map/while/body/eval_jaxpr/tij,trj->tri/dot_general | solution.py:139
  344.4 11.6 %fusion.50 = f32[128,8,128]{2,1,0:T(8,128)} fusion(f32[128,128]{1,0:T(8,128)S(1)} %bitcast.93, f32[128,128]{1,0:T(8,128)} %get-tuple-element.121, f32[128,128]{1,0:T(8,128)S(1)} %bitcast.94, f32[128,128]{1,0:T(8,128)} %get-tuple-element.123, f32[128,128]{1,0:T(8,128)S(1)} %bitcast.92, f32[128,128]{1,0:T(8,128)} %get-tuple-element.125, ...), kind=kOutput, calls=%fused_computation.7.clone.1 | convolution fusion | flops 57016320 | bytes 1704065 | tf_op jit(solution)/shard_map/while/body/eval_jaxpr/tij,trj->tri/dot_general | solution.py:139
  356.6 3.5 gather_fusion
  362.3 11.6 %fusion.50 = f32[128,8,128]{2,1,0:T(8,128)} fusion(f32[128,128]{1,0:T(8,128)S(1)} %bitcast.93, f32[128,128]{1,0:T(8,128)} %get-tuple-element.121, f32[128,128]{1,0:T(8,128)S(1)} %bitcast.94, f32[128,128]{1,0:T(8,128)} %get-tuple-element.123, f32[128,128]{1,0:T(8,128)S(1)} %bitcast.92, f32[128,128]{1,0:T(8,128)} %get-tuple-element.125, ...), kind=kOutput, calls=%fused_computation.7.clone.1 | convolution fusion | flops 57016320 | bytes 1704065 | tf_op jit(solution)/shard_map/while/body/eval_jaxpr/tij,trj->tri/dot_general | solution.py:139
  374.6 3.5 gather_fusion
  380.2 11.6 %fusion.50 = f32[128,8,128]{2,1,0:T(8,128)} fusion(f32[128,128]{1,0:T(8,128)S(1)} %bitcast.93, f32[128,128]{1,0:T(8,128)} %get-tuple-element.121, f32[128,128]{1,0:T(8,128)S(1)} %bitcast.94, f32[128,128]{1,0:T(8,128)} %get-tuple-element.123, f32[128,128]{1,0:T(8,128)S(1)} %bitcast.92, f32[128,128]{1,0:T(8,128)} %get-tuple-element.125, ...), kind=kOutput, calls=%fused_computation.7.clone.1 | convolution fusion | flops 57016320 | bytes 1704065 | tf_op jit(solution)/shard_map/while/body/eval_jaxpr/tij,trj->tri/dot_general | solution.py:139
  392.5 3.5 gather_fusion
  398.1 11.6 %fusion.50 = f32[128,8,128]{2,1,0:T(8,128)} fusion(f32[128,128]{1,0:T(8,128)S(1)} %bitcast.93, f32[128,128]{1,0:T(8,128)} %get-tuple-element.121, f32[128,128]{1,0:T(8,128)S(1)} %bitcast.94, f32[128,128]{1,0:T(8,128)} %get-tuple-element.123, f32[128,128]{1,0:T(8,128)S(1)} %bitcast.92, f32[128,128]{1,0:T(8,128)} %get-tuple-element.125, ...), kind=kOutput, calls=%fused_computation.7.clone.1 | convolution fusion | flops 57016320 | bytes 1704065 | tf_op jit(solution)/shard_map/while/body/eval_jaxpr/tij,trj->tri/dot_general | solution.py:139
  410.4 3.5 gather_fusion
  416.0 11.6 %fusion.50 = f32[128,8,128]{2,1,0:T(8,128)} fusion(f32[128,128]{1,0:T(8,128)S(1)} %bitcast.93, f32[128,128]{1,0:T(8,128)} %get-tuple-element.121, f32[128,128]{1,0:T(8,128)S(1)} %bitcast.94, f32[128,128]{1,0:T(8,128)} %get-tuple-element.123, f32[128,128]{1,0:T(8,128)S(1)} %bitcast.92, f32[128,128]{1,0:T(8,128)} %get-tuple-element.125, ...), kind=kOutput, calls=%fused_computation.7.clone.1 | convolution fusion | flops 57016320 | bytes 1704065 | tf_op jit(solution)/shard_map/while/body/eval_jaxpr/tij,trj->tri/dot_general | solution.py:139
  428.3 3.5 gather_fusion
  433.9 11.6 %fusion.50 = f32[128,8,128]{2,1,0:T(8,128)} fusion(f32[128,128]{1,0:T(8,128)S(1)} %bitcast.93, f32[128,128]{1,0:T(8,128)} %get-tuple-element.121, f32[128,128]{1,0:T(8,128)S(1)} %bitcast.94, f32[128,128]{1,0:T(8,128)} %get-tuple-element.123, f32[128,128]{1,0:T(8,128)S(1)} %bitcast.92, f32[128,128]{1,0:T(8,128)} %get-tuple-element.125, ...), kind=kOutput, calls=%fused_computation.7.clone.1 | convolution fusion | flops 57016320 | bytes 1704065 | tf_op jit(solution)/shard_map/while/body/eval_jaxpr/tij,trj->tri/dot_general | solution.py:139
  451.9 11.6 %fusion.50 = f32[128,8,128]{2,1,0:T(8,128)} fusion(f32[128,128]{1,0:T(8,128)S(1)} %bitcast.93, f32[128,128]{1,0:T(8,128)} %get-tuple-element.121, f32[128,128]{1,0:T(8,128)S(1)} %bitcast.94, f32[128,128]{1,0:T(8,128)} %get-tuple-element.123, f32[128,128]{1,0:T(8,128)S(1)} %bitcast.92, f32[128,128]{1,0:T(8,128)} %get-tuple-element.125, ...), kind=kOutput, calls=%fused_computation.7.clone.1 | convolution fusion | flops 57016320 | bytes 1704065 | tf_op jit(solution)/shard_map/while/body/eval_jaxpr/tij,trj->tri/dot_general | solution.py:139
  469.8 11.6 %fusion.50 = f32[128,8,128]{2,1,0:T(8,128)} fusion(f32[128,128]{1,0:T(8,128)S(1)} %bitcast.93, f32[128,128]{1,0:T(8,128)} %get-tuple-element.121, f32[128,128]{1,0:T(8,128)S(1)} %bitcast.94, f32[128,128]{1,0:T(8,128)} %get-tuple-element.123, f32[128,128]{1,0:T(8,128)S(1)} %bitcast.92, f32[128,128]{1,0:T(8,128)} %get-tuple-element.125, ...), kind=kOutput, calls=%fused_computation.7.clone.1 | convolution fusion | flops 57016320 | bytes 1704065 | tf_op jit(solution)/shard_map/while/body/eval_jaxpr/tij,trj->tri/dot_general | solution.py:139
  487.7 11.6 %fusion.50 = f32[128,8,128]{2,1,0:T(8,128)} fusion(f32[128,128]{1,0:T(8,128)S(1)} %bitcast.93, f32[128,128]{1,0:T(8,128)} %get-tuple-element.121, f32[128,128]{1,0:T(8,128)S(1)} %bitcast.94, f32[128,128]{1,0:T(8,128)} %get-tuple-element.123, f32[128,128]{1,0:T(8,128)S(1)} %bitcast.92, f32[128,128]{1,0:T(8,128)} %get-tuple-element.125, ...), kind=kOutput, calls=%fused_computation.7.clone.1 | convolution fusion | flops 57016320 | bytes 1704065 | tf_op jit(solution)/shard_map/while/body/eval_jaxpr/tij,trj->tri/dot_general | solution.py:139
  500.0 3.5 gather_fusion
  505.6 11.6 %fusion.50 = f32[128,8,128]{2,1,0:T(8,128)} fusion(f32[128,128]{1,0:T(8,128)S(1)} %bitcast.93, f32[128,128]{1,0:T(8,128)} %get-tuple-element.121, f32[128,128]{1,0:T(8,128)S(1)} %bitcast.94, f32[128,128]{1,0:T(8,128)} %get-tuple-element.123, f32[128,128]{1,0:T(8,128)S(1)} %bitcast.92, f32[128,128]{1,0:T(8,128)} %get-tuple-element.125, ...), kind=kOutput, calls=%fused_computation.7.clone.1 | convolution fusion | flops 57016320 | bytes 1704065 | tf_op jit(solution)/shard_map/while/body/eval_jaxpr/tij,trj->tri/dot_general | solution.py:139
  523.5 11.6 %fusion.50 = f32[128,8,128]{2,1,0:T(8,128)} fusion(f32[128,128]{1,0:T(8,128)S(1)} %bitcast.93, f32[128,128]{1,0:T(8,128)} %get-tuple-element.121, f32[128,128]{1,0:T(8,128)S(1)} %bitcast.94, f32[128,128]{1,0:T(8,128)} %get-tuple-element.123, f32[128,128]{1,0:T(8,128)S(1)} %bitcast.92, f32[128,128]{1,0:T(8,128)} %get-tuple-element.125, ...), kind=kOutput, calls=%fused_computation.7.clone.1 | convolution fusion | flops 57016320 | bytes 1704065 | tf_op jit(solution)/shard_map/while/body/eval_jaxpr/tij,trj->tri/dot_general | solution.py:139
  541.4 11.6 %fusion.50 = f32[128,8,128]{2,1,0:T(8,128)} fusion(f32[128,128]{1,0:T(8,128)S(1)} %bitcast.93, f32[128,128]{1,0:T(8,128)} %get-tuple-element.121, f32[128,128]{1,0:T(8,128)S(1)} %bitcast.94, f32[128,128]{1,0:T(8,128)} %get-tuple-element.123, f32[128,128]{1,0:T(8,128)S(1)} %bitcast.92, f32[128,128]{1,0:T(8,128)} %get-tuple-element.125, ...), kind=kOutput, calls=%fused_computation.7.clone.1 | convolution fusion | flops 57016320 | bytes 1704065 | tf_op jit(solution)/shard_map/while/body/eval_jaxpr/tij,trj->tri/dot_general | solution.py:139
  559.4 11.6 %fusion.50 = f32[128,8,128]{2,1,0:T(8,128)} fusion(f32[128,128]{1,0:T(8,128)S(1)} %bitcast.93, f32[128,128]{1,0:T(8,128)} %get-tuple-element.121, f32[128,128]{1,0:T(8,128)S(1)} %bitcast.94, f32[128,128]{1,0:T(8,128)} %get-tuple-element.123, f32[128,128]{1,0:T(8,128)S(1)} %bitcast.92, f32[128,128]{1,0:T(8,128)} %get-tuple-element.125, ...), kind=kOutput, calls=%fused_computation.7.clone.1 | convolution fusion | flops 57016320 | bytes 1704065 | tf_op jit(solution)/shard_map/while/body/eval_jaxpr/tij,trj->tri/dot_general | solution.py:139
  577.3 11.6 %fusion.50 = f32[128,8,128]{2,1,0:T(8,128)} fusion(f32[128,128]{1,0:T(8,128)S(1)} %bitcast.93, f32[128,128]{1,0:T(8,128)} %get-tuple-element.121, f32[128,128]{1,0:T(8,128)S(1)} %bitcast.94, f32[128,128]{1,0:T(8,128)} %get-tuple-element.123, f32[128,128]{1,0:T(8,128)S(1)} %bitcast.92, f32[128,128]{1,0:T(8,128)} %get-tuple-element.125, ...), kind=kOutput, calls=%fused_computation.7.clone.1 | convolution fusion | flops 57016320 | bytes 1704065 | tf_op jit(solution)/shard_map/while/body/eval_jaxpr/tij,trj->tri/dot_general | solution.py:139
  595.2 11.6 %fusion.50 = f32[128,8,128]{2,1,0:T(8,128)} fusion(f32[128,128]{1,0:T(8,128)S(1)} %bitcast.93, f32[128,128]{1,0:T(8,128)} %get-tuple-element.121, f32[128,128]{1,0:T(8,128)S(1)} %bitcast.94, f32[128,128]{1,0:T(8,128)} %get-tuple-element.123, f32[128,128]{1,0:T(8,128)S(1)} %bitcast.92, f32[128,128]{1,0:T(8,128)} %get-tuple-element.125, ...), kind=kOutput, calls=%fused_computation.7.clone.1 | convolution fusion | flops 57016320 | bytes 1704065 | tf_op jit(solution)/shard_map/while/body/eval_jaxpr/tij,trj->tri/dot_general | solution.py:139
  613.1 11.6 %fusion.50 = f32[128,8,128]{2,1,0:T(8,128)} fusion(f32[128,128]{1,0:T(8,128)S(1)} %bitcast.93, f32[128,128]{1,0:T(8,128)} %get-tuple-element.121, f32[128,128]{1,0:T(8,128)S(1)} %bitcast.94, f32[128,128]{1,0:T(8,128)} %get-tuple-element.123, f32[128,128]{1,0:T(8,128)S(1)} %bitcast.92, f32[128,128]{1,0:T(8,128)} %get-tuple-element.125, ...), kind=kOutput, calls=%fused_computation.7.clone.1 | convolution fusion | flops 57016320 | bytes 1704065 | tf_op jit(solution)/shard_map/while/body/eval_jaxpr/tij,trj->tri/dot_general | solution.py:139
  631.0 11.6 %fusion.50 = f32[128,8,128]{2,1,0:T(8,128)} fusion(f32[128,128]{1,0:T(8,128)S(1)} %bitcast.93, f32[128,128]{1,0:T(8,128)} %get-tuple-element.121, f32[128,128]{1,0:T(8,128)S(1)} %bitcast.94, f32[128,128]{1,0:T(8,128)} %get-tuple-element.123, f32[128,128]{1,0:T(8,128)S(1)} %bitcast.92, f32[128,128]{1,0:T(8,128)} %get-tuple-element.125, ...), kind=kOutput, calls=%fused_computation.7.clone.1 | convolution fusion | flops 57016320 | bytes 1704065 | tf_op jit(solution)/shard_map/while/body/eval_jaxpr/tij,trj->tri/dot_general | solution.py:139
  648.9 11.6 %fusion.50 = f32[128,8,128]{2,1,0:T(8,128)} fusion(f32[128,128]{1,0:T(8,128)S(1)} %bitcast.93, f32[128,128]{1,0:T(8,128)} %get-tuple-element.121, f32[128,128]{1,0:T(8,128)S(1)} %bitcast.94, f32[128,128]{1,0:T(8,128)} %get-tuple-element.123, f32[128,128]{1,0:T(8,128)S(1)} %bitcast.92, f32[128,128]{1,0:T(8,128)} %get-tuple-element.125, ...), kind=kOutput, calls=%fused_computation.7.clone.1 | convolution fusion | flops 57016320 | bytes 1704065 | tf_op jit(solution)/shard_map/while/body/eval_jaxpr/tij,trj->tri/dot_general | solution.py:139
  (238 shorter events, 175.0 us)
Async XLA Ops:
  0.0 26.6 %copy-start = (bf16[128,64,128]{2,1,0:T(8,128)(2,1)S(1)}, bf16[128,64,128]{2,1,0:T(8,128)(2,1)}, u32[]{:S(2)}) copy-start(bf16[128,64,128]{2,1,0:T(8,128)(2,1)} %param.19) | copy-start | bytes 6291460
  0.0 12.5 %collective-permute-start = (bf16[128,8,128]{2,1,0:T(8,128)(2,1)}, bf16[128,8,128]{2,1,0:T(8,128)(2,1)}, u32[]{:S(2)}, u32[]{:S(2)}) collective-permute-start(bf16[128,8,128]{2,1,0:T(8,128)(2,1)} %param.15), channel_id=1, source_target_pairs={{0,1},{1,2},{2,3},{3,0},{4,5},{5,6},{6,7},{7,4},{8,9},{9,10},{10,1... | collective-permute-start | bytes 786440 | tf_op jit(solution)/shard_map/ppermute | solution.py:78
  2.1 18.4 %collective-permute-start.1 = (bf16[128,8,128]{2,1,0:T(8,128)(2,1)}, bf16[128,8,128]{2,1,0:T(8,128)(2,1)}, u32[]{:S(2)}, u32[]{:S(2)}) collective-permute-start(bf16[128,8,128]{2,1,0:T(8,128)(2,1)} %param.15), channel_id=1, source_target_pairs={{0,3},{1,0},{2,1},{3,2},{4,7},{5,4},{6,5},{7,6},{8,11},{9,8},{10,9... | collective-permute-start | bytes 786440 | tf_op jit(solution)/shard_map/ppermute | solution.py:85
  12.5 9.0 %collective-permute-start.2 = (bf16[128,8,128]{2,1,0:T(8,128)(2,1)}, bf16[128,8,128]{2,1,0:T(8,128)(2,1)}, u32[]{:S(2)}, u32[]{:S(2)}) collective-permute-start(bf16[128,8,128]{2,1,0:T(8,128)(2,1)} %collective-permute-done), channel_id=1, source_target_pairs={{0,1},{1,2},{2,3},{3,0},{4,5},{5,6},{6,7},{7,4},{8,9},{9,10},{10,1... | collective-permute-start | bytes 786440 | tf_op jit(solution)/shard_map/ppermute | solution.py:78
  24.9 2.9 copy-start.1
  24.9 22.1 %copy-start.2 = (bf16[512,3,128]{2,1,0:T(4,128)(2,1)S(1)}, bf16[512,3,128]{2,1,0:T(4,128)(2,1)}, u32[]{:S(2)}) copy-start(bf16[512,3,128]{2,1,0:T(4,128)(2,1)} %copy.18) | copy-start | bytes 1179652
  28.2 26.6 %copy-start.5 = (bf16[64,64,64]{2,1,0:T(8,128)(2,1)S(1)}, bf16[64,64,64]{2,1,0:T(8,128)(2,1)}, u32[]{:S(2)}) copy-start(bf16[64,64,64]{2,1,0:T(8,128)(2,1)} %param.23) | copy-start | bytes 1572868
  37.6 94.2 %collective-permute-start.5 = (bf16[64,8,64]{2,1,0:T(8,128)(2,1)S(1)}, bf16[64,8,64]{2,1,0:T(8,128)(2,1)}, u32[]{:S(2)}, u32[]{:S(2)}) collective-permute-start(bf16[64,8,64]{2,1,0:T(8,128)(2,1)S(1)} %all_gather.6), channel_id=1, source_target_pairs={{0,4},{4,8},{8,12},{12,16},{16,20},{20,24},{24,28},{28,32},{32,36}... | collective-permute-start | bytes 196616 | tf_op jit(solution)/shard_map/ppermute | solution.py:18
  45.0 86.8 %collective-permute-start.6 = (bf16[64,8,64]{2,1,0:T(8,128)(2,1)S(1)}, bf16[64,8,64]{2,1,0:T(8,128)(2,1)}, u32[]{:S(2)}, u32[]{:S(2)}) collective-permute-start(bf16[64,8,64]{2,1,0:T(8,128)(2,1)S(1)} %all_gather.6), channel_id=1, source_target_pairs={{4,0},{8,4},{12,8},{16,12},{20,16},{24,20},{28,24},{32,28},{36,32}... | collective-permute-start | bytes 196616 | tf_op jit(solution)/shard_map/ppermute | solution.py:20
  49.4 97.1 %collective-permute-start.3 = (bf16[512,11,128]{2,0,1:T(8,128)(2,1)}, bf16[512,11,128]{2,0,1:T(8,128)(2,1)}, u32[]{:S(2)}, u32[]{:S(2)}) collective-permute-start(bf16[512,11,128]{2,0,1:T(8,128)(2,1)} %copy.19), channel_id=1, source_target_pairs={{0,4},{4,8},{8,12},{12,16},{16,20},{20,24},{24,28},{28,32},{32,36}... | collective-permute-start | bytes 4325384 | tf_op jit(solution)/shard_map/ppermute | solution.py:18
  52.9 96.0 %collective-permute-start.4 = (bf16[512,11,128]{2,0,1:T(8,128)(2,1)}, bf16[512,11,128]{2,0,1:T(8,128)(2,1)}, u32[]{:S(2)}, u32[]{:S(2)}) collective-permute-start(bf16[512,11,128]{2,0,1:T(8,128)(2,1)} %copy.19), channel_id=1, source_target_pairs={{4,0},{8,4},{12,8},{16,12},{20,16},{24,20},{28,24},{32,28},{36,32}... | collective-permute-start | bytes 4325384 | tf_op jit(solution)/shard_map/ppermute | solution.py:20
  146.4 4.8 copy-start.3
  176.8 483.7 %copy-start.4 = (f32[128,8,128]{2,1,0:T(8,128)S(1)}, f32[128,8,128]{2,1,0:T(8,128)}, u32[]{:S(2)}) copy-start(f32[128,8,128]{2,1,0:T(8,128)} %fusion.34) | copy-start | bytes 1572868
